TPU v7x, 256 devices: a whole 4x4x8 slice. The times are simulated.
256 devices in a mesh: rows: 8 (over y, core), chan: 32 (over x, z).
Axes of the slice: x: 4, y: 4, z: 8, core: 2. Of those that a mesh axis runs over, the one named last changes fastest.
Arguments:
- features: bfloat16 [512, 1536, 256], P('rows', 'chan'), may hold values from -6 to 6
- mixing: float32 [3, 512, 256], P(None, 'rows'), may hold values from 0 to 1, as said below
- decay_rate: float32 [512, 256], P('rows'), may hold values from 0 to 0.5, as said below
- gate_input: bfloat16 [512, 1536, 256], P('rows', 'chan'), may hold values from -6 to 6
- out_weight: bfloat16 [1536, 1536], replicated, may hold values from -0.15625 to 0.15625
Outputs:
- projected: bfloat16 [512, 1536, 256], P(('rows', 'chan'))
Inputs may be any that keep to these rules, and one draw needn't show every extreme that they name: `mixing`: at every row and column the three weights are positive where their neighbour exists, the left weight is zero at column 0 and the right weight at column 255, and the three sum to one. `decay_rate`: every entry is positive.
All inputs are finite; a program needn't handle non-finite values.
Results may differ from a plain program's by a relative error of at most 0.0049.
Values may be sent and summed in bfloat16 or wider, within the bound.
No kernel may reach another device: no remote copies, remote signals or barrier semaphores. Data moves between devices by JAX's collectives and lax.ppermute only.
A program may use at most 128 MiB of HBM per device.

v0:
```python
import jax
import jax.numpy as jnp
from jax import lax
from jax.sharding import PartitionSpec as P

BLOCK = 16


def entering(part, axis, combine, identity):
    place = lax.axis_index(axis)
    gathered = jax.tree.map(lambda a: lax.all_gather(a, axis), part)
    state = jax.tree.map(lambda a, e: jnp.zeros_like(a) + jnp.asarray(e, a.dtype), part, identity)

    def one(lap, state):
        return combine(
            state, jax.tree.map(lambda a: lax.dynamic_index_in_dim(a, lap, 0, False), gathered)
        )

    return lax.fori_loop(0, place, one, state)


def spread(current, left_w, mid_w, right_w):
    edge_col = jnp.zeros(current.shape[:-1] + (1,), current.dtype)
    before_col = jnp.concatenate([edge_col, current[..., :-1]], axis=-1)
    after_col = jnp.concatenate([current[..., 1:], edge_col], axis=-1)
    return left_w * before_col + mid_w * current + right_w * after_col


def shards(features, mixing, decay_rate, gate_input, out_weight):
    rows_here, channels, col_count = features.shape
    blocks = rows_here // BLOCK
    highest = lax.Precision.HIGHEST
    retain = 1.0 - decay_rate
    weights = retain[None] * mixing
    in_scale = jnp.sqrt(decay_rate)
    forcing = in_scale[:, None, :] * features.astype(jnp.float32)
    coef_steps = weights.reshape(3, blocks, BLOCK, col_count).transpose(2, 0, 1, 3)
    force_steps = forcing.reshape(blocks, BLOCK, channels, col_count).swapaxes(0, 1)
    identity_op = jnp.eye(col_count, dtype=jnp.float32)

    def advance(carry_pair, inputs):
        local_st, op_stack = carry_pair
        coef_row, push_row = inputs
        left_w = coef_row[0][:, None, :]
        mid_w = coef_row[1][:, None, :]
        right_w = coef_row[2][:, None, :]
        local_st = spread(local_st, left_w, mid_w, right_w) + push_row
        op_stack = spread(op_stack, left_w, mid_w, right_w)
        return ((local_st, op_stack), (local_st, op_stack))

    initial = (
        jnp.zeros((blocks, channels, col_count), jnp.float32),
        jnp.broadcast_to(identity_op, (blocks, col_count, col_count)),
    )
    _, (local_all, ops_all) = lax.scan(advance, initial, (coef_steps, force_steps))
    last_ops = ops_all[-1]
    last_local = local_all[-1]

    def carry_on(current, inputs):
        block_op, loc_end = inputs
        return (jnp.dot(current, block_op, precision=highest) + loc_end, current)

    def compose_ops(running, block_op):
        return (jnp.dot(running, block_op, precision=highest), running)

    summary, _ = lax.scan(compose_ops, identity_op, last_ops)
    zero_state = jnp.zeros((channels, col_count), jnp.float32)
    offset, _ = lax.scan(carry_on, zero_state, (last_ops, last_local))

    def compose(earlier, later_pair):
        return (
            jnp.dot(earlier[0], later_pair[0], precision=highest),
            jnp.dot(earlier[1], later_pair[0], precision=highest) + later_pair[1],
        )

    _, incoming = entering((summary, offset), "rows", compose, (identity_op, zero_state))
    _, starts = lax.scan(carry_on, incoming, (last_ops, last_local))
    states = local_all + jnp.einsum("bcv,jbvw->jbcw", starts, ops_all, precision=highest)
    states = states.swapaxes(0, 1).reshape(rows_here, channels, col_count)
    mixed_in = (states * jax.nn.silu(gate_input.astype(jnp.float32))).astype(jnp.bfloat16)
    return jnp.einsum(
        "oc,rcw->row",
        out_weight,
        lax.all_to_all(mixed_in, "chan", split_axis=0, concat_axis=1, tiled=True),
        preferred_element_type=jnp.float32,
    ).astype(jnp.bfloat16)


def solution(mesh):
    in_specs = (
        P("rows", "chan", None),
        P(None, "rows", None),
        P("rows", None),
        P("rows", "chan", None),
        P(),
    )
    out_specs = P(("rows", "chan"), None, None)
    return jax.shard_map(shards, mesh=mesh, in_specs=in_specs, out_specs=out_specs, check_vma=False)
```

profile of v0, /device:TPU:57, one launch (start us, length us, event | category | flops | bytes accessed | tf_op | source)
XLA Modules:
  0.0 202.0 jit_solution(2163504412927207205)
XLA Ops:
  7.6 3.5 %convert_multiply_fusion.1 = f32[64,48,256]{2,1,0:T(8,128)} fusion(bf16[64,48,256]{2,1,0:T(8,128)(2,1)} %param.15, f32[64,256]{1,0:T(8,128)S(1)} %get-tuple-element.273), kind=kLoop, calls=%fused_computation.46 | loop fusion | flops 1572864 | bytes 4784128 | tf_op jit(solution)/shard_map/mul | solution.py:36
  11.2 64.0 %while.65 = (s32[]{:T(128)}, f32[4,48,256]{2,1,0:T(8,128)S(1)}, f32[4,256,256]{2,1,0:T(8,128)S(1)}, f32[16,4,48,256]{3,2,1,0:T(8,128)}, f32[16,4,256,256]{3,2,1,...) while((s32[]{:T(128)}, f32[4,48,256]{2,1,0:T(8,128)S(1)}, ...), condition=%wide.region_1.2_spmd.clone, body=%wide.region_0.1_spmd.clone.sunk | while | flops 1703941 | bytes 11842204 | solution.py:55
  13.5 1.8 bitcast_dynamic-update-slice_fusion.7
  17.5 1.8 bitcast_dynamic-update-slice_fusion.7
  21.4 1.8 bitcast_dynamic-update-slice_fusion.7
  23.6 1.7 bitcast_dynamic-update-slice_fusion.8
  25.4 1.8 bitcast_dynamic-update-slice_fusion.7
  29.4 1.8 bitcast_dynamic-update-slice_fusion.7
  31.6 1.7 bitcast_dynamic-update-slice_fusion.8
  33.4 1.8 bitcast_dynamic-update-slice_fusion.7
  37.4 1.8 bitcast_dynamic-update-slice_fusion.7
  39.6 1.7 bitcast_dynamic-update-slice_fusion.8
  41.5 1.8 bitcast_dynamic-update-slice_fusion.7
  43.6 1.7 bitcast_dynamic-update-slice_fusion.8
  45.5 1.8 bitcast_dynamic-update-slice_fusion.7
  49.5 1.8 bitcast_dynamic-update-slice_fusion.7
  53.5 1.8 bitcast_dynamic-update-slice_fusion.7
  57.5 1.8 bitcast_dynamic-update-slice_fusion.7
  59.7 1.7 bitcast_dynamic-update-slice_fusion.8
  61.5 1.8 bitcast_dynamic-update-slice_fusion.7
  65.5 1.8 bitcast_dynamic-update-slice_fusion.7
  69.5 1.8 bitcast_dynamic-update-slice_fusion.7
  73.5 1.8 bitcast_dynamic-update-slice_fusion.7
  76.6 2.6 %while.62 = (s32[]{:T(128)}, f32[256,256]{0,1:T(8,128)S(1)}, f32[4,256,256]{2,1,0:T(8,128)S(1)}, s32[]{:T(128)}) while((s32[]{:T(128)}, f32[256,256]{0,1:T(8,128)S(1)}, f32[4,256,256]{2,1,0:T(8,128)S(1)}, s32[]{:T(128)}) %tuple.106), condition=%wide.region_3.4_spmd, body=%wide.region_2.3_spmd.sunk | while | flops 201326592 | bytes 1310777 | solution.py:66
  82.2 14.6 %all-gather.1 = f32[384,256]{1,0:T(8,128)} all-gather(f32[48,256]{1,0:T(8,128)S(1)} %get-tuple-element.156), channel_id=3, replica_groups=mesh['rows'=8,'chan'=32] {'rows'}, dimensions={0}, use_global_device_ids=true | all-gather | bytes 442368 | tf_op jit(solution)/shard_map/all_gather | solution.py:11
  96.7 12.7 %all-gather.4.cloned.1.call-done = f32[2048,256]{0,1:T(8,128)} async-done(((f32[256,256]{0,1:T(8,128)}), f32[2048,256]{0,1:T(8,128)}) %all-gather.4.cloned.1.call-update) | async-done | bytes 2097168 | tf_op jit(solution)/shard_map/all_gather | solution.py:11
  109.4 1.9 copy.23
  111.4 7.8 %while.63 = (s32[]{:T(128)}, f32[48,256]{1,0:T(8,128)S(1)}, s32[]{:T(128)}, f32[8,256,256]{2,1,0:T(8,128)S(1)}, f32[8,48,256]{2,1,0:T(8,128)}, /*index=5*/s32[]{:T(128)}, s32[]{:T(128)}, s32[]{:T(128)}) while((s32[]{:T(128)}, f32[48,256]{1,0:T(8,128)S(1)}, s32[]{:T(128)}, f32[8,256,256]{2,1,0:T(8,128)S(1)}, f32[8,48,256]{2,1,0:T(8,128)}, ...), condition=%wide.region_7.8_spmd, body=%wide.region_6.7_spmd.sunk | while | flops 37761028 | bytes 509047 | solution.py:19
  119.2 3.7 %while.64 = (s32[]{:T(128)}, f32[48,256]{1,0:T(8,128)S(1)}, f32[4,48,256]{2,1,0:T(8,128)}, f32[4,256,256]{2,1,0:T(8,128)S(1)}, f32[4,48,256]{2,1,0:T(8,128)S(1)}, /*index=5*/s32[]{:T(128)}) while((s32[]{:T(128)}, f32[48,256]{1,0:T(8,128)S(1)}, f32[4,48,256]{2,1,0:T(8,128)}, f32[4,256,256]{2,1,0:T(8,128)S(1)}, f32[4,48,256]{2,1,0:T(8,128)S(1)}, ...), condition=%wide.region_9.10_spmd, body=%wide.region_8.9_spmd.sunk | while | flops 37761024 | bytes 607813 | solution.py:77
  122.9 14.7 %bitcast_add_fusion.1 = f32[16,4,48,256]{3,2,0,1:T(8,128)S(1)} fusion(f32[16,4,48,256]{3,2,1,0:T(8,128)} %get-tuple-element.153, f32[16,4,256,256]{3,2,1,0:T(8,128)} %get-tuple-element.154, f32[4,48,256]{2,1,0:T(8,128)} %get-tuple-element.158), kind=kOutput, calls=%fused_computation.45 | convolution fusion | flops 2416705536 | bytes 23265280 | tf_op jit(solution)/shard_map/bcv,jbvw->jbcw/dot_general | solution.py:78
  138.7 49.8 %all_to_all.18 = bf16[64,48,256]{2,1,0:T(8,128)(2,1)S(1)} all-to-all(bf16[64,48,256]{2,1,0:T(8,128)(2,1)S(1)} %fusion.27), channel_id=1, replica_groups=mesh['rows'=8,'chan'=32] {'chan'}, dimensions={0} | all-to-all | bytes 3145728 | tf_op jit(solution)/shard_map/all_to_all | solution.py:84
  188.6 5.0 %fusion.31 = bf16[2,1536,256]{1,2,0:T(8,128)(2,1)S(1)} fusion(bf16[2,1536,256]{2,1,0:T(8,128)(2,1)S(1)} %bitcast.133, bf16[1536,1536]{1,0:T(8,128)(2,1)} %param.19), kind=kOutput, calls=%fused_computation.49 | convolution fusion | flops 2416705536 | bytes 7864320 | tf_op jit(solution)/shard_map/oc,rcw->row/dot_general | solution.py:81
  (174 shorter events, 49.2 us)
Async XLA Ops:
  6.5 4.6 %copy-start.2 = (f32[3,64,256]{2,1,0:T(8,128)S(1)}, f32[3,64,256]{2,1,0:T(8,128)}, u32[]{:S(2)}) copy-start(f32[3,64,256]{2,1,0:T(8,128)} %param.16) | copy-start | bytes 589828
  6.5 102.9 %all-gather.4.cloned.1.call-start = ((), (), s32[]{:S(2)}) async-start(), calls=%async_computation.1 | async-start | bytes 2359296 | tf_op jit(solution)/shard_map/all_gather | solution.py:11
  79.2 0.7 copy-start
  122.9 14.7 %copy-start.1 = (bf16[64,48,256]{2,1,0:T(8,128)(2,1)S(1)}, bf16[64,48,256]{2,1,0:T(8,128)(2,1)}, u32[]{:S(2)}) copy-start(bf16[64,48,256]{2,1,0:T(8,128)(2,1)} %param.18) | copy-start | bytes 4718596
Sparse Core Ops, SparseCore 0:
  80.1 29.3 all-gather.3
where the time goes:
time: 203 us; the launch traced here: 202 us
  blocking collectives  64.3 us (32%)
  other arithmetic  61.3 us (30%)
  matrix products  31.8 us (16%)
  local copies, waits for them, and re-layouts  17.2 us (8%)
  between operations  13.6 us (7%)
  waiting for transfers between devices  12.7 us (6%)
    dynamic_update_slice x32, other arithmetic, shards(): lax.scan(advance, initial, (coef_steps, force_steps))  55.5 us
    all_to_all x1, blocking collectives, shards(): lax.all_to_all(mixed_in, 'chan', split_axis=0, concat_axis=1, tiled=True)  49.8 us
    dot_general x1, matrix products, shards(): jnp.einsum('bcv,jbvw->jbcw', starts, ops_all, precision=highest)  14.7 us
    all_gather x1, blocking collectives, entering(): gathered = jax.tree.map(lambda a: lax.all_gather(a, axis), part)  14.6 us
    all_gather x1, waiting for transfers between devices, entering(): gathered = jax.tree.map(lambda a: lax.all_gather(a, axis), part)  12.7 us
    dot_general x7, matrix products, compose(): jnp.dot(earlier[1], later_pair[0], precision=highest) + later_pair[1]  7.51 us
    slice x32, local copies, waits for them, and re-layouts, spread(): before_col = jnp.concatenate([edge_col, current[..., :-1]], axis=-1)  7.43 us
    dot_general x1, matrix products, shards(): jnp.einsum('oc,rcw->row', out_weight, lax.all_to_all(mixed_in, 'chan', sp...  4.99 us
  transfers between devices with their start and end apart: 1, of which 1 were waited for; matrix products, arithmetic and copies ran while one was open for 1% of the time, Pallas kernels for 0%

commit v1 on v0

--- a/solution.py
+++ b/solution.py
@@ -4,6 +4,13 @@
 from jax.sharding import PartitionSpec as P
 
 BLOCK = 16
+
+
+def trade_parts(block, mesh_axis, split, join):
+    n_dev = lax.axis_size(mesh_axis)
+    pieces = jnp.stack(jnp.split(block, n_dev, axis=split), axis=0)
+    pieces = lax.all_to_all(pieces, mesh_axis, split_axis=0, concat_axis=0)
+    return jnp.concatenate(pieces, axis=join)
 
 
 def entering(part, axis, combine, identity):
@@ -81,7 +88,7 @@
     return jnp.einsum(
         "oc,rcw->row",
         out_weight,
-        lax.all_to_all(mixed_in, "chan", split_axis=0, concat_axis=1, tiled=True),
+        trade_parts(mixed_in, "chan", 0, 1),
         preferred_element_type=jnp.float32,
     ).astype(jnp.bfloat16)
 

time: 203 us -> 201 us (level)
  matrix products: 31.8 us -> 29.4 us
    dot_general x1, matrix products: 4.99 us -> 2.65 us  [shards(): jnp.einsum('oc,rcw->row', out_weight, trade_parts(mixed_in, 'chan', 0, 1)...]
where the time goes in v1:
time: 201 us; the launch traced here: 200 us
  blocking collectives  64.3 us (32%)
  other arithmetic  61.3 us (30%)
  matrix products  29.4 us (15%)
  local copies, waits for them, and re-layouts  17.3 us (9%)
  between operations  13.9 us (7%)
  waiting for transfers between devices  12.7 us (6%)
    dynamic_update_slice x32, other arithmetic, shards(): lax.scan(advance, initial, (coef_steps, force_steps))  55.5 us
    all_to_all x1, blocking collectives, trade_parts(): pieces = lax.all_to_all(pieces, mesh_axis, split_axis=0, concat_axis=0)  49.8 us
    dot_general x1, matrix products, shards(): jnp.einsum('bcv,jbvw->jbcw', starts, ops_all, precision=highest)  14.7 us
    all_gather x1, blocking collectives, entering(): gathered = jax.tree.map(lambda a: lax.all_gather(a, axis), part)  14.6 us
    all_gather x1, waiting for transfers between devices, entering(): gathered = jax.tree.map(lambda a: lax.all_gather(a, axis), part)  12.7 us
    dot_general x7, matrix products, compose(): jnp.dot(earlier[1], later_pair[0], precision=highest) + later_pair[1]  7.51 us
    slice x32, local copies, waits for them, and re-layouts, spread(): before_col = jnp.concatenate([edge_col, current[..., :-1]], axis=-1)  7.43 us
  transfers between devices with their start and end apart: 1, of which 1 were waited for; matrix products, arithmetic and copies ran while one was open for 1% of the time, Pallas kernels for 0%

profile of v1, /device:TPU:57, one launch (start us, length us, event | category | flops | bytes accessed | tf_op | source)
XLA Modules:
  0.0 200.2 jit_solution(16299586019483769999)
XLA Ops:
  7.6 3.5 %convert_multiply_fusion.1 = f32[64,48,256]{2,1,0:T(8,128)} fusion(bf16[64,48,256]{2,1,0:T(8,128)(2,1)} %param.15, f32[64,256]{1,0:T(8,128)S(1)} %get-tuple-element.273), kind=kLoop, calls=%fused_computation.46 | loop fusion | flops 1572864 | bytes 4784128 | tf_op jit(solution)/shard_map/mul | solution.py:43
  11.3 64.0 %while.65 = (s32[]{:T(128)}, f32[4,48,256]{2,1,0:T(8,128)S(1)}, f32[4,256,256]{2,1,0:T(8,128)S(1)}, f32[16,4,48,256]{3,2,1,0:T(8,128)}, f32[16,4,256,256]{3,2,1,...) while((s32[]{:T(128)}, f32[4,48,256]{2,1,0:T(8,128)S(1)}, ...), condition=%wide.region_1.2_spmd.clone, body=%wide.region_0.1_spmd.clone.sunk | while | flops 1703941 | bytes 11842204 | solution.py:62
  13.5 1.8 bitcast_dynamic-update-slice_fusion.7
  17.5 1.8 bitcast_dynamic-update-slice_fusion.7
  21.4 1.8 bitcast_dynamic-update-slice_fusion.7
  25.4 1.8 bitcast_dynamic-update-slice_fusion.7
  29.4 1.8 bitcast_dynamic-update-slice_fusion.7
  33.4 1.8 bitcast_dynamic-update-slice_fusion.7
  37.3 1.8 bitcast_dynamic-update-slice_fusion.7
  39.5 1.7 bitcast_dynamic-update-slice_fusion.8
  41.4 1.8 bitcast_dynamic-update-slice_fusion.7
  43.6 1.8 bitcast_dynamic-update-slice_fusion.8
  45.5 1.8 bitcast_dynamic-update-slice_fusion.7
  47.7 1.7 bitcast_dynamic-update-slice_fusion.8
  49.5 1.8 bitcast_dynamic-update-slice_fusion.7
  53.5 1.8 bitcast_dynamic-update-slice_fusion.7
  55.7 1.7 bitcast_dynamic-update-slice_fusion.8
  57.5 1.8 bitcast_dynamic-update-slice_fusion.7
  59.7 1.7 bitcast_dynamic-update-slice_fusion.8
  61.5 1.8 bitcast_dynamic-update-slice_fusion.7
  65.5 1.8 bitcast_dynamic-update-slice_fusion.7
  69.5 1.8 bitcast_dynamic-update-slice_fusion.7
  73.5 1.8 bitcast_dynamic-update-slice_fusion.7
  76.6 2.6 %while.62 = (s32[]{:T(128)}, f32[256,256]{0,1:T(8,128)S(1)}, f32[4,256,256]{2,1,0:T(8,128)S(1)}, s32[]{:T(128)}) while((s32[]{:T(128)}, f32[256,256]{0,1:T(8,128)S(1)}, f32[4,256,256]{2,1,0:T(8,128)S(1)}, s32[]{:T(128)}) %tuple.106), condition=%wide.region_3.4_spmd, body=%wide.region_2.3_spmd.sunk | while | flops 201326592 | bytes 1310777 | solution.py:73
  82.2 14.6 %all-gather.1 = f32[384,256]{1,0:T(8,128)} all-gather(f32[48,256]{1,0:T(8,128)S(1)} %get-tuple-element.156), channel_id=3, replica_groups=mesh['rows'=8,'chan'=32] {'rows'}, dimensions={0}, use_global_device_ids=true | all-gather | bytes 442368 | tf_op jit(solution)/shard_map/all_gather | solution.py:18
  96.7 12.7 %all-gather.4.cloned.1.call-done = f32[2048,256]{0,1:T(8,128)} async-done(((f32[256,256]{0,1:T(8,128)}), f32[2048,256]{0,1:T(8,128)}) %all-gather.4.cloned.1.call-update) | async-done | bytes 2097168 | tf_op jit(solution)/shard_map/all_gather | solution.py:18
  109.4 1.9 copy.54
  111.4 7.8 %while.63 = (s32[]{:T(128)}, f32[48,256]{1,0:T(8,128)S(1)}, s32[]{:T(128)}, f32[8,256,256]{2,1,0:T(8,128)S(1)}, f32[8,48,256]{2,1,0:T(8,128)}, /*index=5*/s32[]{:T(128)}, s32[]{:T(128)}, s32[]{:T(128)}) while((s32[]{:T(128)}, f32[48,256]{1,0:T(8,128)S(1)}, s32[]{:T(128)}, f32[8,256,256]{2,1,0:T(8,128)S(1)}, f32[8,48,256]{2,1,0:T(8,128)}, ...), condition=%wide.region_7.8_spmd, body=%wide.region_6.7_spmd.sunk | while | flops 37761028 | bytes 509047 | solution.py:26
  119.2 3.7 %while.64 = (s32[]{:T(128)}, f32[48,256]{1,0:T(8,128)S(1)}, f32[4,48,256]{2,1,0:T(8,128)}, f32[4,256,256]{2,1,0:T(8,128)S(1)}, f32[4,48,256]{2,1,0:T(8,128)S(1)}, /*index=5*/s32[]{:T(128)}) while((s32[]{:T(128)}, f32[48,256]{1,0:T(8,128)S(1)}, f32[4,48,256]{2,1,0:T(8,128)}, f32[4,256,256]{2,1,0:T(8,128)S(1)}, f32[4,48,256]{2,1,0:T(8,128)S(1)}, ...), condition=%wide.region_9.10_spmd, body=%wide.region_8.9_spmd.sunk | while | flops 37761024 | bytes 607813 | solution.py:84
  122.9 14.7 %bitcast_add_fusion.1 = f32[16,4,48,256]{3,2,0,1:T(8,128)S(1)} fusion(f32[16,4,48,256]{3,2,1,0:T(8,128)} %get-tuple-element.153, f32[16,4,256,256]{3,2,1,0:T(8,128)} %get-tuple-element.154, f32[4,48,256]{2,1,0:T(8,128)} %get-tuple-element.158), kind=kOutput, calls=%fused_computation.45 | convolution fusion | flops 2416705536 | bytes 23265280 | tf_op jit(solution)/shard_map/bcv,jbvw->jbcw/dot_general | solution.py:85
  139.2 49.8 %all_to_all.5 = bf16[32,2,48,256]{3,2,1,0:T(8,128)(2,1)S(1)} all-to-all(bf16[32,2,48,256]{3,2,1,0:T(8,128)(2,1)S(1)} %constant_dynamic-update-slice_fusion), channel_id=1, replica_groups=mesh['rows'=8,'chan'=32] {'chan'}, dimensions={0} | all-to-all | bytes 3145728 | tf_op jit(solution)/shard_map/all_to_all | solution.py:12
  189.1 2.7 %fusion.31 = bf16[2,1536,256]{1,2,0:T(8,128)(2,1)S(1)} fusion(bf16[2,1536,256]{2,1,0:T(8,128)(2,1)S(1)} %bitcast.259, bf16[1536,1536]{1,0:T(8,128)(2,1)S(1)} %bitcast.265), kind=kOutput, calls=%fused_computation.49 | convolution fusion | flops 2416705536 | bytes 7864320 | tf_op jit(solution)/shard_map/oc,rcw->row/dot_general | solution.py:88
  (211 shorter events, 49.3 us)
Async XLA Ops:
  6.5 102.9 %all-gather.4.cloned.1.call-start = ((), (), s32[]{:S(2)}) async-start(), calls=%async_computation.1 | async-start | bytes 2359296 | tf_op jit(solution)/shard_map/all_gather | solution.py:18
  7.6 3.6 %copy-start.2 = (f32[3,64,256]{2,1,0:T(8,128)S(1)}, f32[3,64,256]{2,1,0:T(8,128)}, u32[]{:S(2)}) copy-start(f32[3,64,256]{2,1,0:T(8,128)} %param.16) | copy-start | bytes 589828
  79.2 0.7 copy-start
  122.9 14.7 %copy-start.1 = (bf16[64,48,256]{2,1,0:T(8,128)(2,1)S(1)}, bf16[64,48,256]{2,1,0:T(8,128)(2,1)}, u32[]{:S(2)}) copy-start(bf16[64,48,256]{2,1,0:T(8,128)(2,1)} %param.18) | copy-start | bytes 4718596
  137.6 51.4 %slice-start = ((s8[4718592]{0:T(1024)(128)(4,1)}), s8[4194304]{0:T(1024)(128)(4,1)S(1)}, s32[]{:S(2)}) async-start(s8[4718592]{0:T(1024)(128)(4,1)} %bitcast.264), calls=%async_computation.2 | async-start | bytes 8388608
  139.0 50.1 %slice-start.1 = ((s8[4718592]{0:T(1024)(128)(4,1)}), s8[524288]{0:T(1024)(128)(4,1)S(1)}, s32[]{:S(2)}) async-start(s8[4718592]{0:T(1024)(128)(4,1)} %bitcast.264), calls=%async_computation.3 | async-start | bytes 1048576
Sparse Core Ops, SparseCore 0:
  80.1 29.3 all-gather.3
